TPU v7x, 512 devices: a whole 4x8x8 slice. The times are simulated.
512 devices in a mesh: seq: 64 (over x, y, core), head: 8 (over z).
Axes of the slice: x: 4, y: 8, z: 8, core: 2. Of those that a mesh axis runs over, the one named last changes fastest.
Arguments:
- queries: bfloat16 [69632, 2048], P('seq', 'head'), may hold values from -50 to 50
- keys: bfloat16 [69632, 2048], P('seq', 'head'), may hold values from -6 to 6
- values: bfloat16 [69632, 2048], P('seq', 'head'), may hold values from -48 to 48
- rand_group: int32 [1088, 3], replicated, may hold values from 0 to 63, all different within a row; in each aligned block of 17 rows (0 to 16, 17 to 33, ...) at most 2 rows name the same one
- rand_offset: int32 [1088, 3], replicated, may hold values from 0 to 16
- glob_blocks: int32 [2], replicated, may hold values from 0 to 1087
- w_out: bfloat16 [2048, 4096], P(None, 'head'), may hold values from -0.125 to 0.125
Outputs:
- layer_out: bfloat16 [69632, 4096], P('seq', 'head')
Inputs may be any that keep to these rules, and one draw needn't show every extreme that they name: `rand_group`: each row names 3 different groups. Among the 17 rows of one aligned block of 17 rows, no group is named more than 2 times, and in every draw some group is named exactly 2 times in some such block.
All inputs are finite; a program needn't handle non-finite values.
Results may differ from a plain program's by a relative error of at most 0.0056.
Values may be sent and summed in bfloat16 or wider, within the bound.
A program may use at most 128 MiB of HBM per device.

v0:
```python
from functools import reduce
import math
import jax
import jax.numpy as jnp
from jax import lax
from jax.sharding import PartitionSpec as P

DH = 128
BLOCK = 64
R = 3
G = 2


def padded_2(x, sides, width):
    for axis, dim in sides:
        size, length = (lax.axis_size(axis), x.shape[dim])
        up = [(i, (i + 1) % size) for i in range(size)]
        down = [(j, i) for i, j in up]
        last = lax.slice_in_dim(x, length - width, length, axis=dim)
        initial = lax.slice_in_dim(x, 0, width, axis=dim)
        before = lax.ppermute(last, axis, up)
        after = lax.ppermute(initial, axis, down)
        x = jnp.concatenate([before, x, after], axis=dim)
    return x


def spread(block, axis, holder):
    block = jnp.where(lax.axis_index(axis) == holder, block, jnp.zeros_like(block))
    return lax.psum(block, axis)


def attend_sets(query_rows, pair_sets, columns):
    head_count = columns // DH
    block_count = query_rows.shape[0]
    query_heads = query_rows.reshape(block_count, BLOCK, head_count, DH)
    score_scale = 1.0 / math.sqrt(DH)
    score_list = []
    for pair_rows in pair_sets:
        key_part = pair_rows[..., :columns].reshape(block_count, -1, head_count, DH)
        score_list.append(
            jnp.einsum("nqhd,nkhd->nhqk", query_heads, key_part, preferred_element_type=jnp.float32)
            * score_scale
        )
    row_max = reduce(
        jnp.maximum, [jnp.max(score_part, axis=-1, keepdims=True) for score_part in score_list]
    )
    row_total = jnp.zeros((block_count, head_count, BLOCK), jnp.float32)
    weighted = jnp.zeros((block_count, BLOCK, head_count, DH), jnp.float32)
    for score_part, pair_rows in zip(score_list, pair_sets):
        weights = jnp.exp(score_part - row_max)
        row_total = jnp.sum(weights, axis=-1)
        value_part = pair_rows[..., columns:].reshape(block_count, -1, head_count, DH)
        weighted = jnp.einsum(
            "nhqk,nkhd->nqhd",
            weights.astype(jnp.bfloat16),
            value_part,
            preferred_element_type=jnp.float32,
        )
    context = weighted / jnp.transpose(row_total, (0, 2, 1))[..., None]
    return context.astype(jnp.bfloat16).reshape(block_count * BLOCK, columns)


def on_device(queries, keys, values, rand_group, rand_offset, glob_blocks, w_out):
    columns = queries.shape[1]
    tokens_dev = queries.shape[0]
    per_device = tokens_dev // BLOCK
    seq_count = lax.axis_size("seq")
    my_index = lax.axis_index("seq")
    slot_cap = rand_group.shape[0] // seq_count * R
    slot_cap = max(2, (slot_cap + seq_count - 1) // seq_count)
    pair_rows = jnp.concatenate([keys, values], axis=1)
    pair_blocks = pair_rows.reshape(per_device, BLOCK, 2 * columns)
    padded = padded_2(pair_rows, (("seq", 0),), BLOCK)
    padded_blocks = padded.reshape(per_device + 2, BLOCK, 2 * columns)
    window_sets = jnp.stack([padded_blocks[:-2], padded_blocks[1:-1], padded_blocks[2:]], axis=1)
    found = []
    for global_slot in range(G):
        owner_index = glob_blocks[global_slot] // per_device
        local_spot = glob_blocks[global_slot] % per_device
        piece_rows = lax.dynamic_index_in_dim(pair_blocks, local_spot, 0, keepdims=False)
        found.append(spread(piece_rows, "seq", owner_index))
    global_pairs = jnp.stack(found)
    global_sets = jnp.broadcast_to(global_pairs[None], (per_device, G, BLOCK, 2 * columns))
    request_count = per_device * R
    asked_groups = rand_group.reshape(seq_count, request_count)
    asked_offsets = rand_offset.reshape(seq_count, request_count)
    asked_here = (asked_groups == my_index).astype(jnp.int32)
    slot_rank = jnp.cumsum(asked_here, axis=1) - asked_here
    slot_index = jnp.arange(slot_cap, dtype=jnp.int32)
    slot_match = (asked_here[:, None, :] == 1) & (
        slot_rank[:, None, :] == slot_index[None, :, None]
    )
    send_spot = jnp.sum(jnp.where(slot_match, asked_offsets[:, None, :], 0), axis=2)
    slot_filled = jnp.any(slot_match, axis=2)
    outgoing = jnp.take(pair_blocks, send_spot.reshape(-1), axis=0).reshape(
        seq_count, slot_cap, BLOCK, 2 * columns
    )
    outgoing = jnp.where(slot_filled[:, :, None, None], outgoing, jnp.zeros_like(outgoing))
    incoming = lax.all_to_all(outgoing, "seq", split_axis=0, concat_axis=0, tiled=True)
    my_groups = lax.dynamic_slice_in_dim(rand_group, my_index * per_device, per_device, 0).reshape(
        -1
    )
    request_index = jnp.arange(request_count, dtype=jnp.int32)
    earlier_same = (my_groups[None, :] == my_groups[:, None]) & (
        request_index[None, :] < request_index[:, None]
    )
    arrival_rank = jnp.sum(earlier_same.astype(jnp.int32), axis=1)
    arrival_spot = my_groups * slot_cap + arrival_rank
    random_sets = jnp.take(
        incoming.reshape(seq_count * slot_cap, BLOCK, 2 * columns), arrival_spot, axis=0
    )
    random_sets = random_sets.reshape(per_device, R, BLOCK, 2 * columns)
    query_rows = queries.reshape(per_device, BLOCK, columns)
    joined_sets = jnp.concatenate([window_sets, global_sets, random_sets], axis=1).reshape(
        per_device, -1, 2 * columns
    )
    context = attend_sets(query_rows, [joined_sets], columns)
    summed = jnp.dot(
        lax.all_gather(context, "head", axis=1, tiled=True),
        w_out,
        preferred_element_type=jnp.float32,
    )
    return summed.astype(jnp.bfloat16)


def solution(mesh):
    return jax.shard_map(
        on_device,
        mesh=mesh,
        in_specs=(
            P("seq", "head"),
            P("seq", "head"),
            P("seq", "head"),
            P(),
            P(),
            P(),
            P(None, "head"),
        ),
        out_specs=P("seq", "head"),
        check_vma=False,
    )
```

profile of v0, /device:TPU:64, one launch (start us, length us, event | category | flops | bytes accessed | tf_op | source)
XLA Modules:
  0.0 396.6 jit_solution(1737452305502771908)
XLA Ops:
  8.3 1.0 copy.58
  9.8 1.1 constant_dynamic-update-slice_fusion.1
  11.3 1.1 constant_dynamic-update-slice_fusion
  12.4 6.4 %gather_fusion = bf16[128,64,512]{2,1,0:T(8,128)(2,1)} fusion(bf16[17,64,512]{2,1,0:T(8,128)(2,1)S(1)} %bitcast.52, s32[1024]{0:T(1024)S(1)} %pad_clamp_fusion.1), kind=kCustom, calls=%fused_computation | custom fusion | bytes 16777728 | tf_op jit(solution)/shard_map/jit(_take)/gather | solution.py:95
  18.8 7.5 %select_select_fusion = bf16[64,2,64,512]{3,2,1,0:T(8,128)(2,1)} fusion(bf16[64,2,64,512]{3,2,1,0:T(8,128)(2,1)} %bitcast.55, pred[64,2]{1,0:T(8,128)(4,1)S(1)} %copy.60, pred[64,2]{1,0:T(8,128)(4,1)S(1)} %copy.57), kind=kLoop, calls=%fused_computation.2 | loop fusion | flops 8388608 | bytes 16777472 | tf_op jit(solution)/shard_map/jit(_where)/select_n | solution.py:98
  26.3 10.9 %all-to-all-start = ((bf16[64,2,64,512]{3,2,1,0:T(8,128)(2,1)}), bf16[64,2,64,512]{3,2,1,0:T(8,128)(2,1)}, u32[]{:S(2)}, u32[]{:S(2)}) async-start(bf16[64,2,64,512]{3,2,1,0:T(8,128)(2,1)} %select_select_fusion), calls=%async_computation | async-start | bytes 16777216 | tf_op jit(solution)/shard_map/all_to_all | solution.py:99
  37.3 1.9 collective-permute-start
  39.2 7.0 %collective-permute-start.1 = (bf16[64,512]{1,0:T(8,128)(2,1)S(1)}, bf16[64,512]{1,0:T(8,128)(2,1)S(1)}, u32[]{:S(2)}, u32[]{:S(2)}) collective-permute-start(bf16[64,512]{1,0:T(8,128)(2,1)S(1)} %get-tuple-element.15), channel_id=1, source_target_pairs={{8,0},{16,8},{24,16},{32,24},{40,32},{48,40},{56,48},{64,56},{72,6... | collective-permute-start | bytes 196616 | tf_op jit(solution)/shard_map/ppermute | solution.py:22
  53.0 2.5 reshape_reshape.3
  55.5 213.7 %all-reduce.3.cloned.1.call-done = (bf16[1,64,512]{2,1,0:T(8,128)(2,1)}, bf16[1,64,512]{2,1,0:T(8,128)(2,1)}) async-done(((bf16[1,64,512]{2,1,0:T(8,128)(2,1)}, bf16[1,64,512]{2,1,0:T(8,128)(2,1)}), (bf16[1,64,512]{2,1,0:T(8,128)(2,1)}, bf16[1,64,512]{2,1,0:T(8,128)(2,1)})) %all-reduce.3.cloned.1.call-update) | async-done | bytes 131088 | tf_op jit(solution)/shard_map/psum | solution.py:29
  270.3 1.1 constant_dynamic-update-slice_fusion.4
  271.4 1.1 constant_dynamic-update-slice_fusion.3
  272.4 1.1 constant_dynamic-update-slice_fusion.2
  273.5 1.7 broadcast_dynamic-update-slice_fusion
  275.2 5.9 %gather_fusion.1 = bf16[51,64,512]{2,1,0:T(8,128)(2,1)} fusion(bf16[128,64,512]{2,1,0:T(8,128)(2,1)} %bitcast.12, s32[1024]{0:T(1024)S(1)} %pad_clamp_fusion), kind=kCustom, calls=%fused_computation.1 | custom fusion | bytes 6684876 | tf_op jit(solution)/shard_map/jit(_take)/gather | solution.py:109
  281.1 5.2 %select_dynamic-update-slice_fusion = bf16[17,8,64,512]{3,2,1,0:T(8,128)(2,1)} fusion(bf16[17,8,64,512]{3,2,1,0:T(8,128)(2,1)} %broadcast_dynamic-update-slice_fusion, bf16[17,3,64,512]{3,2,1,0:T(8,128)(2,1)} %bitcast.57, pred[17,3]{1,0:T(8,128)(4,1)S(1)} %copy.52), kind=kLoop, calls=%fused_computation.8 | loop fusion | flops 1671168 | bytes 6684723 | tf_op jit(solution)/shard_map/concatenate | solution.py:114
  286.2 8.1 %fusion.19 = (bf16[17,512,256]{2,1,0:T(8,128)(2,1)}, bf16[17,512,256]{2,1,0:T(8,128)(2,1)}) fusion(bf16[17,512,512]{2,1,0:T(8,128)(2,1)} %bitcast.16), kind=kLoop, calls=%fused_computation.51 | loop fusion | bytes 17825792 | tf_op jit(solution)/shard_map/slice | solution.py:39
  294.3 6.5 %copy.64 = bf16[17,512,256]{1,2,0:T(8,128)(2,1)} copy(bf16[17,512,256]{2,1,0:T(8,128)(2,1)} %get-tuple-element.9) | data formatting | bytes 8912896 | tf_op jit(solution)/shard_map/slice | solution.py:39
  300.8 6.6 %copy.63 = bf16[17,512,256]{1,2,0:T(8,128)(2,1)} copy(bf16[17,512,256]{2,1,0:T(8,128)(2,1)} %get-tuple-element.10) | data formatting | bytes 8912896 | tf_op jit(solution)/shard_map/slice | solution.py:52
  307.5 3.4 bitcast_reduce_fusion
  310.9 1.3 fusion.1
  312.2 2.0 divide_convert_fusion
  315.8 68.3 %all-gather.2.cloned.1.call-done = bf16[1088,2048]{1,0:T(8,128)(2,1)} async-done(((bf16[1088,256]{1,0:T(8,128)(2,1)}), bf16[1088,2048]{1,0:T(8,128)(2,1)}) %all-gather.2.cloned.1.call-update) | async-done | bytes 4456464 | tf_op jit(solution)/shard_map/all_gather | solution.py:119
  384.1 5.7 %convolution_convert_fusion = bf16[1088,512]{1,0:T(8,128)(2,1)} fusion(bf16[1088,2048]{1,0:T(8,128)(2,1)} %all-gather.2.cloned.1.call-done, bf16[2048,512]{1,0:T(8,128)(2,1)S(1)} %copy-done), kind=kOutput, calls=%fused_computation.9 | convolution fusion | flops 2282258432 | bytes 7667712 | tf_op jit(solution)/shard_map/dot_general | solution.py:118
  (56 shorter events, 8.4 us)
Async XLA Ops:
  6.5 377.5 %copy-start = (bf16[2048,512]{1,0:T(8,128)(2,1)S(1)}, bf16[2048,512]{1,0:T(8,128)(2,1)}, u32[]{:S(2)}) copy-start(bf16[2048,512]{1,0:T(8,128)(2,1)} %param.13) | copy-start | bytes 6291460
  26.3 19.9 %copy-start.2 = (s32[2]{0:T(128)S(1)}, s32[2]{0:T(128)}, u32[]{:S(2)}) copy-start(s32[2]{0:T(128)} %param.12) | copy-start | bytes 28
  26.3 248.9 %all-to-all-start = ((bf16[64,2,64,512]{3,2,1,0:T(8,128)(2,1)}), bf16[64,2,64,512]{3,2,1,0:T(8,128)(2,1)}, u32[]{:S(2)}, u32[]{:S(2)}) async-start(bf16[64,2,64,512]{3,2,1,0:T(8,128)(2,1)} %select_select_fusion), calls=%async_computation | async-start | bytes 16777216 | tf_op jit(solution)/shard_map/all_to_all | solution.py:99
  37.2 232.0 %all-reduce.3.cloned.1.call-start = ((), (), s32[]{:S(2)}) async-start(), calls=%async_computation.2 | async-start | bytes 262144 | tf_op jit(solution)/shard_map/psum | solution.py:29
  37.3 232.8 %collective-permute-start = (bf16[64,512]{1,0:T(8,128)(2,1)S(1)}, bf16[64,512]{1,0:T(8,128)(2,1)S(1)}, u32[]{:S(2)}, u32[]{:S(2)}) collective-permute-start(bf16[64,512]{1,0:T(8,128)(2,1)S(1)} %get-tuple-element.16), channel_id=1, source_target_pairs={{0,8},{8,16},{16,24},{24,32},{32,40},{40,48},{48,56},{56,64},{64,7... | collective-permute-start | bytes 196616 | tf_op jit(solution)/shard_map/ppermute | solution.py:21
  39.2 230.9 %collective-permute-start.1 = (bf16[64,512]{1,0:T(8,128)(2,1)S(1)}, bf16[64,512]{1,0:T(8,128)(2,1)S(1)}, u32[]{:S(2)}, u32[]{:S(2)}) collective-permute-start(bf16[64,512]{1,0:T(8,128)(2,1)S(1)} %get-tuple-element.15), channel_id=1, source_target_pairs={{8,0},{16,8},{24,16},{32,24},{40,32},{48,40},{56,48},{64,56},{72,6... | collective-permute-start | bytes 196616 | tf_op jit(solution)/shard_map/ppermute | solution.py:22
  51.2 332.9 %all-gather.2.cloned.1.call-start = ((), (), s32[]{:S(2)}) async-start(), calls=%async_computation.1 | async-start | bytes 5013504 | tf_op jit(solution)/shard_map/all_gather | solution.py:119
  300.8 6.6 %copy-start.1 = (bf16[17,64,2,128]{3,2,1,0:T(2,128)(2,1)S(1)}, bf16[17,64,2,128]{3,2,1,0:T(2,128)(2,1)}, u32[]{:S(2)}) copy-start(bf16[17,64,2,128]{3,2,1,0:T(2,128)(2,1)} %reshape_reshape.3) | copy-start | bytes 1671172
  307.4 4.8 %slice-start = ((s8[4456448]{0:T(1024)(128)(4,1)}), s8[4194304]{0:T(1024)(128)(4,1)S(1)}, s32[]{:S(2)}) async-start(s8[4456448]{0:T(1024)(128)(4,1)} %bitcast.58), calls=%async_computation.3 | async-start | bytes 8388608
  307.5 4.8 %slice-start.1 = ((s8[4456448]{0:T(1024)(128)(4,1)}), s8[262144]{0:T(1024)(128)(4,1)S(1)}, s32[]{:S(2)}) async-start(s8[4456448]{0:T(1024)(128)(4,1)} %bitcast.58), calls=%async_computation.4 | async-start | bytes 524288
Sparse Core Ops, SparseCore 0:
  51.3 217.8 all-reduce.2
  315.9 68.1 all-gather.1
where the time goes:
time: 398 us; the launch traced here: 397 us
  waiting for transfers between devices  282 us (71%)
  local copies, waits for them, and re-layouts  48.1 us (12%)
  starting transfers between devices  20.1 us (5%)
  other arithmetic  17.9 us (4%)
  between operations  17.3 us (4%)
  matrix products  11.2 us (3%)
    psum x1, waiting for transfers between devices, spread(): return lax.psum(block, axis)  214 us
    all_gather x1, waiting for transfers between devices, on_device(): lax.all_gather(context, 'head', axis=1, tiled=True)  68.3 us
    slice x2, local copies, waits for them, and re-layouts, attend_sets(): key_part = pair_rows[..., :columns].reshape(block_count, -1, head_count, DH)  14.6 us
    all_to_all x1, starting transfers between devices, on_device(): lax.all_to_all(outgoing, 'seq', split_axis=0, concat_axis=0, tiled=True)  10.9 us
  transfers between devices with their start and end apart: 5, of which 2 were waited for; matrix products, arithmetic and copies ran while one was open for 3% of the time, Pallas kernels for 0%

commit v1 on v0

--- a/solution.py
+++ b/solution.py
@@ -115,11 +115,11 @@
         per_device, -1, 2 * columns
     )
     context = attend_sets(query_rows, [joined_sets], columns)
-    summed = jnp.dot(
-        lax.all_gather(context, "head", axis=1, tiled=True),
-        w_out,
-        preferred_element_type=jnp.float32,
+    meet_the_node = lambda inner_x, at_axis: jnp.concatenate(
+        jax.lax.all_to_all(jnp.stack([inner_x] * jax.lax.axis_size("head"), 0), "head", 0, 0),
+        at_axis,
     )
+    summed = jnp.dot(meet_the_node(context, at_axis=1), w_out, preferred_element_type=jnp.float32)
     return summed.astype(jnp.bfloat16)
 
 

time: 398 us -> 439 us (1.10)
  the two profiles are of different devices: /device:TPU:64 before, /device:TPU:1 now
where the time goes in v1:
time: 439 us; the launch traced here: 438 us
  waiting for transfers between devices  219 us (50%)
  blocking collectives  109 us (25%)
  local copies, waits for them, and re-layouts  48.3 us (11%)
  other arithmetic  17.9 us (4%)
  starting transfers between devices  17.8 us (4%)
  between operations  17.6 us (4%)
  matrix products  8.89 us (2%)
    psum x1, waiting for transfers between devices, spread(): return lax.psum(block, axis)  219 us
    all_to_all x1, blocking collectives, on_device(): jax.lax.all_to_all(jnp.stack([inner_x] * jax.lax.axis_size('head'), 0), '...  109 us
    slice x2, local copies, waits for them, and re-layouts, attend_sets(): key_part = pair_rows[..., :columns].reshape(block_count, -1, head_count, DH)  14.6 us
    all_to_all x1, starting transfers between devices, on_device(): lax.all_to_all(outgoing, 'seq', split_axis=0, concat_axis=0, tiled=True)  12.1 us
  transfers between devices with their start and end apart: 4, of which 1 were waited for; matrix products, arithmetic and copies ran while one was open for 3% of the time, Pallas kernels for 0%

profile of v1, /device:TPU:1, one launch (start us, length us, event | category | flops | bytes accessed | tf_op | source)
XLA Modules:
  0.0 438.3 jit_solution(7799335994730859243)
XLA Ops:
  8.3 1.0 copy.69
  9.8 1.1 constant_dynamic-update-slice_fusion.1
  11.3 1.1 constant_dynamic-update-slice_fusion
  12.4 6.4 %gather_fusion = bf16[128,64,512]{2,1,0:T(8,128)(2,1)} fusion(bf16[17,64,512]{2,1,0:T(8,128)(2,1)S(1)} %bitcast.55, s32[1024]{0:T(1024)S(1)} %pad_clamp_fusion.1), kind=kCustom, calls=%fused_computation | custom fusion | bytes 16777728 | tf_op jit(solution)/shard_map/jit(_take)/gather | solution.py:95
  18.8 7.5 %select_select_fusion = bf16[64,2,64,512]{3,2,1,0:T(8,128)(2,1)} fusion(bf16[64,2,64,512]{3,2,1,0:T(8,128)(2,1)} %bitcast.58, pred[64,2]{1,0:T(8,128)(4,1)S(1)} %copy.71, pred[64,2]{1,0:T(8,128)(4,1)S(1)} %copy.68), kind=kLoop, calls=%fused_computation.2 | loop fusion | flops 8388608 | bytes 16777472 | tf_op jit(solution)/shard_map/jit(_where)/select_n | solution.py:98
  26.3 12.1 %all-to-all-start = ((bf16[64,2,64,512]{3,2,1,0:T(8,128)(2,1)}), bf16[64,2,64,512]{3,2,1,0:T(8,128)(2,1)}, u32[]{:S(2)}, u32[]{:S(2)}) async-start(bf16[64,2,64,512]{3,2,1,0:T(8,128)(2,1)} %select_select_fusion), calls=%async_computation | async-start | bytes 16777216 | tf_op jit(solution)/shard_map/all_to_all | solution.py:99
  38.5 3.5 collective-permute-start
  42.0 2.1 collective-permute-start.1
  51.0 2.5 reshape_reshape.3
  53.5 218.6 %all-reduce.3.cloned.1.call-done = (bf16[1,64,512]{2,1,0:T(8,128)(2,1)}, bf16[1,64,512]{2,1,0:T(8,128)(2,1)}) async-done(((bf16[1,64,512]{2,1,0:T(8,128)(2,1)}, bf16[1,64,512]{2,1,0:T(8,128)(2,1)}), (bf16[1,64,512]{2,1,0:T(8,128)(2,1)}, bf16[1,64,512]{2,1,0:T(8,128)(2,1)})) %all-reduce.3.cloned.1.call-update) | async-done | bytes 131088 | tf_op jit(solution)/shard_map/psum | solution.py:29
  273.2 1.1 constant_dynamic-update-slice_fusion.4
  274.3 1.1 constant_dynamic-update-slice_fusion.3
  275.4 1.1 constant_dynamic-update-slice_fusion.2
  276.5 1.6 broadcast_dynamic-update-slice_fusion
  278.1 5.9 %gather_fusion.1 = bf16[51,64,512]{2,1,0:T(8,128)(2,1)} fusion(bf16[128,64,512]{2,1,0:T(8,128)(2,1)} %bitcast.12, s32[1024]{0:T(1024)S(1)} %pad_clamp_fusion), kind=kCustom, calls=%fused_computation.1 | custom fusion | bytes 6684876 | tf_op jit(solution)/shard_map/jit(_take)/gather | solution.py:109
  284.1 5.1 %select_dynamic-update-slice_fusion = bf16[17,8,64,512]{3,2,1,0:T(8,128)(2,1)} fusion(bf16[17,8,64,512]{3,2,1,0:T(8,128)(2,1)} %broadcast_dynamic-update-slice_fusion, bf16[17,3,64,512]{3,2,1,0:T(8,128)(2,1)} %bitcast.61, pred[17,3]{1,0:T(8,128)(4,1)S(1)} %copy.63), kind=kLoop, calls=%fused_computation.8 | loop fusion | flops 1671168 | bytes 6684723 | tf_op jit(solution)/shard_map/concatenate | solution.py:114
  289.2 8.1 %fusion.19 = (bf16[17,512,256]{2,1,0:T(8,128)(2,1)}, bf16[17,512,256]{2,1,0:T(8,128)(2,1)}) fusion(bf16[17,512,512]{2,1,0:T(8,128)(2,1)} %bitcast.16), kind=kLoop, calls=%fused_computation.51 | loop fusion | bytes 17825792 | tf_op jit(solution)/shard_map/slice | solution.py:39
  297.3 6.5 %copy.75 = bf16[17,512,256]{1,2,0:T(8,128)(2,1)} copy(bf16[17,512,256]{2,1,0:T(8,128)(2,1)} %get-tuple-element.9) | data formatting | bytes 8912896 | tf_op jit(solution)/shard_map/slice | solution.py:39
  303.8 6.6 %copy.74 = bf16[17,512,256]{1,2,0:T(8,128)(2,1)} copy(bf16[17,512,256]{2,1,0:T(8,128)(2,1)} %get-tuple-element.10) | data formatting | bytes 8912896 | tf_op jit(solution)/shard_map/slice | solution.py:52
  310.4 3.4 bitcast_reduce_fusion
  313.8 1.3 fusion.1
  315.2 2.0 divide_convert_fusion
  318.2 109.2 %all_to_all.10 = bf16[8,1088,256]{2,1,0:T(8,128)(2,1)S(1)} all-to-all(bf16[8,1088,256]{2,1,0:T(8,128)(2,1)S(1)} %stack.27), channel_id=1, replica_groups=mesh['seq'=64,'head'=8] {'head'}, dimensions={0} | all-to-all | bytes 8912896 | tf_op jit(solution)/shard_map/all_to_all | solution.py:119
  428.0 3.5 convolution_convert_fusion
  (56 shorter events, 8.3 us)
Async XLA Ops:
  6.5 421.4 %copy-start = (bf16[2048,512]{1,0:T(8,128)(2,1)S(1)}, bf16[2048,512]{1,0:T(8,128)(2,1)}, u32[]{:S(2)}) copy-start(bf16[2048,512]{1,0:T(8,128)(2,1)} %param.13) | copy-start | bytes 6291460
  26.3 17.9 %copy-start.2 = (s32[2]{0:T(128)S(1)}, s32[2]{0:T(128)}, u32[]{:S(2)}) copy-start(s32[2]{0:T(128)} %param.12) | copy-start | bytes 28
  26.3 251.8 %all-to-all-start = ((bf16[64,2,64,512]{3,2,1,0:T(8,128)(2,1)}), bf16[64,2,64,512]{3,2,1,0:T(8,128)(2,1)}, u32[]{:S(2)}, u32[]{:S(2)}) async-start(bf16[64,2,64,512]{3,2,1,0:T(8,128)(2,1)} %select_select_fusion), calls=%async_computation | async-start | bytes 16777216 | tf_op jit(solution)/shard_map/all_to_all | solution.py:99
  38.4 233.7 %all-reduce.3.cloned.1.call-start = ((), (), s32[]{:S(2)}) async-start(), calls=%async_computation.2 | async-start | bytes 262144 | tf_op jit(solution)/shard_map/psum | solution.py:29
  38.5 234.6 %collective-permute-start = (bf16[64,512]{1,0:T(8,128)(2,1)S(1)}, bf16[64,512]{1,0:T(8,128)(2,1)S(1)}, u32[]{:S(2)}, u32[]{:S(2)}) collective-permute-start(bf16[64,512]{1,0:T(8,128)(2,1)S(1)} %get-tuple-element.16), channel_id=1, source_target_pairs={{0,8},{8,16},{16,24},{24,32},{32,40},{40,48},{48,56},{56,64},{64,7... | collective-permute-start | bytes 196616 | tf_op jit(solution)/shard_map/ppermute | solution.py:21
  42.0 231.0 %collective-permute-start.1 = (bf16[64,512]{1,0:T(8,128)(2,1)S(1)}, bf16[64,512]{1,0:T(8,128)(2,1)S(1)}, u32[]{:S(2)}, u32[]{:S(2)}) collective-permute-start(bf16[64,512]{1,0:T(8,128)(2,1)S(1)} %get-tuple-element.15), channel_id=1, source_target_pairs={{8,0},{16,8},{24,16},{32,24},{40,32},{48,40},{56,48},{64,56},{72,6... | collective-permute-start | bytes 196616 | tf_op jit(solution)/shard_map/ppermute | solution.py:22
  303.8 6.6 %copy-start.1 = (bf16[17,64,2,128]{3,2,1,0:T(2,128)(2,1)S(1)}, bf16[17,64,2,128]{3,2,1,0:T(2,128)(2,1)}, u32[]{:S(2)}) copy-start(bf16[17,64,2,128]{3,2,1,0:T(2,128)(2,1)} %reshape_reshape.3) | copy-start | bytes 1671172
  310.4 4.7 %slice-start = ((s8[4456448]{0:T(1024)(128)(4,1)}), s8[4194304]{0:T(1024)(128)(4,1)S(1)}, s32[]{:S(2)}) async-start(s8[4456448]{0:T(1024)(128)(4,1)} %bitcast.62), calls=%async_computation.3 | async-start | bytes 8388608
  310.4 4.8 %slice-start.1 = ((s8[4456448]{0:T(1024)(128)(4,1)}), s8[262144]{0:T(1024)(128)(4,1)S(1)}, s32[]{:S(2)}) async-start(s8[4456448]{0:T(1024)(128)(4,1)} %bitcast.62), calls=%async_computation.4 | async-start | bytes 524288
Sparse Core Ops, SparseCore 0:
  49.5 222.5 all-reduce.2
